TPU v7x, 32 devices: a whole 2x2x4 slice. The times are simulated.
32 devices in a mesh: agent: 8 (over y, x, core), res: 4 (over z).
Axes of the slice: x: 2, y: 2, z: 4, core: 2. Of those that a mesh axis runs over, the one named last changes fastest.
Arguments:
- linear_cost: float32 [2048, 2048], P('agent', 'res'), may hold values from -6 to 6
- agent_type: int32 [2048], P('agent'), may hold values from 0 to 3, as said below
- block_mask: int32 [2048, 16], P('agent', 'res'), may hold values 0 or 1
- inverses: bfloat16 [4, 2048, 2048], P(None, 'res'), as said below
- cost_weight: float32 [2048], P('res'), may hold values from 0.5 to 8
- target: float32 [2048], P('res'), may hold values from -6 to 6
Outputs:
- usage: float32 [2048, 2048], P('agent', 'res')
- shared: float32 [2048], P('res')
- prices: float32 [2048], P('res')
- primal_norm: float32 [5], replicated
- dual_norm: float32 [5], replicated
Inputs may be any that keep to these rules, and one draw needn't show every extreme that they name: Each inverses[k] is exactly symmetric: inverses[k, i, j] equals inverses[k, j, i]. `agent_type`: each aligned block of 256 agents (the agents held by one device along the agent axis) holds exactly 64 agents of each type, in no particular order.
All inputs are finite; a program needn't handle non-finite values. No bound on the sum of `block_mask` on one device may be relied on, other than what follows from the above.
Results may differ from a plain program's by a relative error of at most 0.0039.
Values may be sent and summed in bfloat16 or wider, within the bound.
No kernel may reach another device: no remote copies, remote signals or barrier semaphores. Data moves between devices by JAX's collectives and lax.ppermute only.
A program may use at most 64 MiB of HBM per device.

v0:
```python
import jax
import jax.numpy as jnp
from jax import lax
from jax.sharding import PartitionSpec as P

BLK = 128
ITERS = 5
penalty = 1.0
eps = 1e-06


def on_device(linear_cost, agent_type, block_mask, inverses, cost_weight, target):
    local_agents, local_width = linear_cost.shape
    type_count = inverses.shape[0]
    group_rows = local_agents // type_count
    count = local_agents * lax.axis_size("agent")
    block_count = block_mask.shape[1]
    order = jnp.argsort(agent_type, stable=True)
    restore = jnp.argsort(order, stable=True)
    expand = jnp.broadcast_to(
        block_mask.astype(jnp.float32)[:, :, None], (local_agents, block_count, BLK)
    ).reshape(local_agents, local_width)
    usage = jnp.zeros(linear_cost.shape, jnp.float32)
    mean_usage = jnp.zeros((local_width,), jnp.float32)
    shared = jnp.zeros((local_width,), jnp.float32)
    prices = jnp.zeros((local_width,), jnp.float32)
    primal_list = []
    dual_list = []
    for iteration in range(ITERS):
        rhs = (penalty * (usage - mean_usage + shared - prices) - linear_cost).astype(jnp.bfloat16)
        grouped = rhs[order].reshape(type_count, group_rows, local_width)
        product = jnp.einsum(
            "tas,tws->taw",
            lax.all_gather(grouped, "res", axis=2, tiled=True),
            inverses,
            preferred_element_type=jnp.float32,
        )
        new_usage = product.reshape(local_agents, local_width)[restore]
        new_usage = new_usage * expand
        change_local = penalty * penalty * jnp.sum((new_usage - usage) ** 2)
        usage = new_usage
        column_sum = jnp.sum(usage, axis=0)
        usage_sum = lax.psum(column_sum, "agent")
        dual2 = lax.psum(change_local, ("agent", "res"))
        mean_usage = usage_sum / count
        shared = (cost_weight * target + penalty * (prices + mean_usage)) / (cost_weight + penalty)
        prices = prices + mean_usage - shared
        primal2 = lax.psum(count * jnp.sum((mean_usage - shared) ** 2), "res")
        primal_list.append(jnp.sqrt(primal2 + eps))
        dual_list.append(jnp.sqrt(dual2 + eps))
    primal_norm = jnp.stack(primal_list)
    dual_norm = jnp.stack(dual_list)
    return (usage, shared, prices, primal_norm, dual_norm)


def solution(mesh):
    placed = (
        P("agent", "res"),
        P("agent"),
        P("agent", "res"),
        P(None, "res", None),
        P("res"),
        P("res"),
    )
    return jax.shard_map(
        on_device,
        mesh=mesh,
        in_specs=placed,
        out_specs=(P("agent", "res"), P("res"), P("res"), P(), P()),
        check_vma=False,
    )
```

profile of v0, /device:TPU:12, one launch (start us, length us, event | category | flops | bytes accessed | tf_op | source)
XLA Modules:
  0.0 334.9 jit_solution(6932095263842248031)
XLA Ops:
  7.2 0.0 all-gather.6.cloned.1.call-start
  7.2 3.8 %sort.31 = (s32[256]{0:T(256)}, s32[256]{0:T(256)S(1)}) sort(s32[256]{0:T(256)} %param.7, s32[256]{0:T(256)S(1)} %iota.7), dimensions={0}, to_apply=%region_0.0 | sort | flops 2048 | bytes 4096 | tf_op jit(solution)/shard_map/jit(argsort)/sort | solution.py:18
  11.1 1.1 subtract_convert_fusion.4
  12.2 1.9 gather_fusion
  14.0 0.0 all-gather.6.cloned.1.call-update
  14.0 0.0 all-gather.8.cloned.1.call-start
  14.1 3.2 sort.32
  17.3 0.7 convert_element_type.19
  18.0 0.1 copy.11
  18.1 0.0 copy-start.1
  18.1 0.0 copy-start.3
  18.1 0.0 copy-start
  18.2 25.1 %all-gather.6.cloned.1.call-done = bf16[4,64,2048]{2,1,0:T(8,128)(2,1)} async-done(((bf16[4,64,512]{2,1,0:T(8,128)(2,1)}), bf16[4,64,2048]{2,1,0:T(8,128)(2,1)}) %all-gather.6.cloned.1.call-update) | async-done | bytes 1048592 | tf_op jit(solution)/shard_map/all_gather | solution.py:34
  43.3 6.4 %fusion.13 = f32[4,64,512]{2,1,0:T(8,128)S(1)} fusion(bf16[4,64,2048]{2,1,0:T(8,128)(2,1)} %all-gather.6.cloned.1.call-done, bf16[4,512,2048]{2,1,0:T(8,128)(2,1)} %param.9), kind=kOutput, calls=%fused_computation.56 | convolution fusion | flops 536870912 | bytes 9961472 | tf_op jit(solution)/shard_map/tas,tws->taw/dot_general | solution.py:32
  49.7 1.0 gather_fusion.1
  50.7 0.3 broadcast_in_dim.11
  51.0 0.1 fusion.12
  51.1 11.9 %psum.105 = f32[512]{0:T(512)S(1)} all-reduce(f32[512]{0:T(512)S(1)} %get-tuple-element.44), channel_id=1, replica_groups=mesh['agent'=8,'res'=4] {'agent'}, use_global_device_ids=true, to_apply=%region_3.4 | all-reduce | flops 512 | bytes 4096 | tf_op jit(solution)/shard_map/psum | solution.py:43
  63.0 0.0 copy-done.3
  63.0 0.6 multiply_reduce_fusion.9
  63.6 0.1 subtract_convert_fusion.3
  63.7 1.9 gather_fusion.2
  65.6 0.0 all-gather.8.cloned.1.call-update
  65.6 0.0 all-gather.10.cloned.1.call-start
  65.7 27.5 %all-gather.8.cloned.1.call-done = bf16[4,64,2048]{2,1,0:T(8,128)(2,1)} async-done(((bf16[4,64,512]{2,1,0:T(8,128)(2,1)}), bf16[4,64,2048]{2,1,0:T(8,128)(2,1)}) %all-gather.8.cloned.1.call-update) | async-done | bytes 1048592 | tf_op jit(solution)/shard_map/all_gather | solution.py:34
  93.1 6.4 %fusion.14 = f32[4,64,512]{2,1,0:T(8,128)S(1)} fusion(bf16[4,64,2048]{2,1,0:T(8,128)(2,1)} %all-gather.8.cloned.1.call-done, bf16[4,512,2048]{2,1,0:T(8,128)(2,1)} %param.9), kind=kOutput, calls=%fused_computation.57 | convolution fusion | flops 536870912 | bytes 9961472 | tf_op jit(solution)/shard_map/tas,tws->taw/dot_general | solution.py:32
  99.5 1.0 gather_fusion.3
  100.5 0.1 fusion.11
  100.6 11.9 %psum.106 = f32[512]{0:T(512)S(1)} all-reduce(f32[512]{0:T(512)S(1)} %get-tuple-element.42), channel_id=1, replica_groups=mesh['agent'=8,'res'=4] {'agent'}, use_global_device_ids=true, to_apply=%region_5.6 | all-reduce | flops 512 | bytes 4096 | tf_op jit(solution)/shard_map/psum | solution.py:43
  112.5 0.6 multiply_reduce_fusion.8
  113.1 0.1 subtract_convert_fusion.2
  113.2 1.9 gather_fusion.4
  115.0 0.0 all-gather.10.cloned.1.call-update
  115.1 0.0 all-gather.12.cloned.1.call-start
  115.1 27.5 %all-gather.10.cloned.1.call-done = bf16[4,64,2048]{2,1,0:T(8,128)(2,1)} async-done(((bf16[4,64,512]{2,1,0:T(8,128)(2,1)}), bf16[4,64,2048]{2,1,0:T(8,128)(2,1)}) %all-gather.10.cloned.1.call-update) | async-done | bytes 1048592 | tf_op jit(solution)/shard_map/all_gather | solution.py:34
  142.6 6.4 %fusion.15 = f32[4,64,512]{2,1,0:T(8,128)S(1)} fusion(bf16[4,64,2048]{2,1,0:T(8,128)(2,1)} %all-gather.10.cloned.1.call-done, bf16[4,512,2048]{2,1,0:T(8,128)(2,1)} %param.9), kind=kOutput, calls=%fused_computation.58 | convolution fusion | flops 536870912 | bytes 9961472 | tf_op jit(solution)/shard_map/tas,tws->taw/dot_general | solution.py:32
  148.9 1.0 gather_fusion.5
  149.9 0.1 fusion.10
  150.0 12.1 %psum.107 = f32[512]{0:T(512)S(1)} all-reduce(f32[512]{0:T(512)S(1)} %get-tuple-element.40), channel_id=1, replica_groups=mesh['agent'=8,'res'=4] {'agent'}, use_global_device_ids=true, to_apply=%region_7.8 | all-reduce | flops 512 | bytes 4096 | tf_op jit(solution)/shard_map/psum | solution.py:43
  162.1 0.6 multiply_reduce_fusion.7
  162.7 0.1 subtract_convert_fusion.1
  162.8 1.9 gather_fusion.6
  164.7 0.0 all-gather.12.cloned.1.call-update
  164.7 0.0 all-gather.14.cloned.1.call-start
  164.8 27.4 %all-gather.12.cloned.1.call-done = bf16[4,64,2048]{2,1,0:T(8,128)(2,1)} async-done(((bf16[4,64,512]{2,1,0:T(8,128)(2,1)}), bf16[4,64,2048]{2,1,0:T(8,128)(2,1)}) %all-gather.12.cloned.1.call-update) | async-done | bytes 1048592 | tf_op jit(solution)/shard_map/all_gather | solution.py:34
  192.2 6.4 %fusion.16 = f32[4,64,512]{2,1,0:T(8,128)S(1)} fusion(bf16[4,64,2048]{2,1,0:T(8,128)(2,1)} %all-gather.12.cloned.1.call-done, bf16[4,512,2048]{2,1,0:T(8,128)(2,1)} %param.9), kind=kOutput, calls=%fused_computation.59 | convolution fusion | flops 536870912 | bytes 9961472 | tf_op jit(solution)/shard_map/tas,tws->taw/dot_general | solution.py:32
  198.6 1.8 gather_fusion.7
  200.4 1.2 fusion.9
  201.5 11.9 %psum.108 = f32[512]{0:T(512)S(1)} all-reduce(f32[512]{0:T(512)S(1)} %get-tuple-element.38), channel_id=1, replica_groups=mesh['agent'=8,'res'=4] {'agent'}, use_global_device_ids=true, to_apply=%region_9.10 | all-reduce | flops 512 | bytes 4096 | tf_op jit(solution)/shard_map/psum | solution.py:43
  213.4 0.6 multiply_reduce_fusion.6
  214.0 0.1 subtract_convert_fusion
  214.1 1.9 gather_fusion.8
  216.0 0.0 all-gather.14.cloned.1.call-update
  218.6 24.9 %all-gather.14.cloned.1.call-done = bf16[4,64,2048]{2,1,0:T(8,128)(2,1)} async-done(((bf16[4,64,512]{2,1,0:T(8,128)(2,1)}), bf16[4,64,2048]{2,1,0:T(8,128)(2,1)}) %all-gather.14.cloned.1.call-update) | async-done | bytes 1048592 | tf_op jit(solution)/shard_map/all_gather | solution.py:34
  243.5 6.4 %fusion.17 = f32[4,64,512]{2,1,0:T(8,128)S(1)} fusion(bf16[4,64,2048]{2,1,0:T(8,128)(2,1)} %all-gather.14.cloned.1.call-done, bf16[4,512,2048]{2,1,0:T(8,128)(2,1)} %param.9), kind=kOutput, calls=%fused_computation.60 | convolution fusion | flops 536870912 | bytes 9961472 | tf_op jit(solution)/shard_map/tas,tws->taw/dot_general | solution.py:32
  249.9 1.8 gather_fusion.9
  251.7 2.8 multiply_reduce_fusion
  254.5 11.9 %psum.109 = f32[512]{0:T(512)S(1)} all-reduce(f32[512]{0:T(512)S(1)} %get-tuple-element.14), channel_id=1, replica_groups=mesh['agent'=8,'res'=4] {'agent'}, use_global_device_ids=true, to_apply=%region_11.12 | all-reduce | flops 512 | bytes 4096 | tf_op jit(solution)/shard_map/psum | solution.py:43
  266.3 0.6 multiply_reduce_fusion.5
  267.6 0.6 fusion
  268.2 9.8 %all-reduce.1 = (f32[]{:T(128)}, f32[]{:T(128)}, f32[]{:T(128)}, f32[]{:T(128)}, f32[]{:T(128)}) all-reduce(f32[]{:T(128)S(6)} %mul.99, f32[]{:T(128)S(6)} %mul.100, f32[]{:T(128)S(6)} %mul.101, f32[]{:T(128)S(6)} %mul.102, f32[]{:T(128)S(6)} %mul.103), channel_id=1, replica_groups=mesh['agent'=8,'res'=4] {'res'}, use_global_device_ids=true, to_apply=%region_13.14 | all-reduce | flops 5 | bytes 40 | tf_op jit(solution)/shard_map/psum | solution.py:48
  281.3 42.5 %all-reduce = (f32[]{:T(128)}, f32[]{:T(128)}, f32[]{:T(128)}, f32[]{:T(128)}, f32[]{:T(128)}) all-reduce(f32[]{:T(128)} %get-tuple-element.13, f32[]{:T(128)} %get-tuple-element.12, f32[]{:T(128)} %get-tuple-element.11, f32[]{:T(128)} %get-tuple-element.10, f32[]{:T(128)} %get-tuple-element.9), channel_id=1, replica_groups=mesh['agent'=8,'res'=4] {'agent','res'}, use_global_device_ids=true, to_apply=%region_23.24 | all-reduce | flops 5 | bytes 40 | tf_op jit(solution)/shard_map/psum | solution.py:44
  327.2 0.6 stack.41
  327.8 0.6 stack.47
  (13 shorter events, 0.0 us)
Async XLA Ops:
  7.2 36.1 %all-gather.6.cloned.1.call-start = ((), (), s32[]{:S(2)}) async-start(), calls=%async_computation | async-start | bytes 1310720 | tf_op jit(solution)/shard_map/all_gather | solution.py:34
  14.0 79.1 %all-gather.8.cloned.1.call-start = ((), (), s32[]{:S(2)}) async-start(), calls=%async_computation.1 | async-start | bytes 1310720 | tf_op jit(solution)/shard_map/all_gather | solution.py:34
  18.1 44.9 %copy-start.1 = (f32[512]{0:T(512)S(1)}, f32[512]{0:T(512)}, u32[]{:S(2)}) copy-start(f32[512]{0:T(512)} %param.10) | copy-start | bytes 6148
  18.1 44.9 %copy-start.3 = (f32[512]{0:T(512)S(1)}, f32[512]{0:T(512)}, u32[]{:S(2)}) copy-start(f32[512]{0:T(512)} %param.11) | copy-start | bytes 6148
  18.1 45.5 %copy-start = (f32[256,512]{1,0:T(8,128)S(1)}, f32[256,512]{1,0:T(8,128)}, u32[]{:S(2)}) copy-start(f32[256,512]{1,0:T(8,128)} %param.6) | copy-start | bytes 1572868
  65.6 77.0 %all-gather.10.cloned.1.call-start = ((), (), s32[]{:S(2)}) async-start(), calls=%async_computation.2 | async-start | bytes 1310720 | tf_op jit(solution)/shard_map/all_gather | solution.py:34
  115.1 77.2 %all-gather.12.cloned.1.call-start = ((), (), s32[]{:S(2)}) async-start(), calls=%async_computation.3 | async-start | bytes 1310720 | tf_op jit(solution)/shard_map/all_gather | solution.py:34
  164.7 78.8 %all-gather.14.cloned.1.call-start = ((), (), s32[]{:S(2)}) async-start(), calls=%async_computation.4 | async-start | bytes 1310720 | tf_op jit(solution)/shard_map/all_gather | solution.py:34
  267.0 61.4 %copy-start.2 = (f32[512]{0:T(512)}, f32[512]{0:T(512)S(1)}, u32[]{:S(2)}) copy-start(f32[512]{0:T(512)S(1)} %get-tuple-element.26) | copy-start | bytes 6148
Sparse Core Ops, SparseCore 0:
  14.2 29.0 all-gather.5
  65.7 27.3 all-gather.7
  115.2 27.3 all-gather.9
  164.8 27.3 all-gather.11
  216.1 27.3 all-gather.13
where the time goes:
time: 336 us; the launch traced here: 335 us
  waiting for transfers between devices  132 us (39%)
  blocking collectives  112 us (33%)
  matrix products  31.9 us (9%)
  between operations  23.8 us (7%)
  local copies, waits for them, and re-layouts  17.4 us (5%)
  other arithmetic  17.3 us (5%)
    all_gather x5, waiting for transfers between devices, on_device(): lax.all_gather(grouped, 'res', axis=2, tiled=True)  132 us
    psum x5, blocking collectives, on_device(): usage_sum = lax.psum(column_sum, 'agent')  59.6 us
    psum x1, blocking collectives, on_device(): dual2 = lax.psum(change_local, ('agent', 'res'))  42.5 us
    dot_general x5, matrix products, on_device(): jnp.einsum('tas,tws->taw', lax.all_gather(grouped, 'res', axis=2, tiled=T...  31.9 us
    psum x1, blocking collectives, on_device(): primal2 = lax.psum(count * jnp.sum((mean_usage - shared) ** 2), 'res')  9.78 us
    gather x5, local copies, waits for them, and re-layouts, on_device(): grouped = rhs[order].reshape(type_count, group_rows, local_width)  9.27 us
  transfers between devices with their start and end apart: 5, of which 5 were waited for; matrix products, arithmetic and copies ran while one was open for 1% of the time, Pallas kernels for 0%

commit v1 on v0

--- a/solution.py
+++ b/solution.py
@@ -41,7 +41,7 @@
         usage = new_usage
         column_sum = jnp.sum(usage, axis=0)
         usage_sum = lax.psum(column_sum, "agent")
-        dual2 = lax.psum(change_local, ("agent", "res"))
+        dual2 = lax.psum(lax.psum(change_local, "agent"), "res")
         mean_usage = usage_sum / count
         shared = (cost_weight * target + penalty * (prices + mean_usage)) / (cost_weight + penalty)
         prices = prices + mean_usage - shared

time: 336 us -> 299 us (0.89); the launches traced: 335 us -> 294 us
  blocking collectives: 112 us -> 70.5 us
    psum x1 -> x0, blocking collectives: 42.5 us -> none  [on_device(): dual2 = lax.psum(change_local, ('agent', 'res'))]
where the time goes in v1:
time: 299 us; the launch traced here: 294 us
  waiting for transfers between devices  132 us (44%)
  blocking collectives  70.5 us (24%)
  matrix products  31.9 us (11%)
  between operations  23.8 us (8%)
  local copies, waits for them, and re-layouts  17.4 us (6%)
  other arithmetic  17.2 us (6%)
    all_gather x5, waiting for transfers between devices, on_device(): lax.all_gather(grouped, 'res', axis=2, tiled=True)  132 us
    psum x5, blocking collectives, on_device(): usage_sum = lax.psum(column_sum, 'agent')  60.5 us
    dot_general x5, matrix products, on_device(): jnp.einsum('tas,tws->taw', lax.all_gather(grouped, 'res', axis=2, tiled=T...  31.9 us
    psum x1, blocking collectives, on_device(): primal2 = lax.psum(count * jnp.sum((mean_usage - shared) ** 2), 'res')  10 us
    gather x5, local copies, waits for them, and re-layouts, on_device(): grouped = rhs[order].reshape(type_count, group_rows, local_width)  9.27 us
    gather x5, local copies, waits for them, and re-layouts, on_device(): new_usage = product.reshape(local_agents, local_width)[restore]  6.45 us
  transfers between devices with their start and end apart: 5, of which 5 were waited for; matrix products, arithmetic and copies ran while one was open for 1% of the time, Pallas kernels for 0%

profile of v1, /device:TPU:12, one launch (start us, length us, event | category | flops | bytes accessed | tf_op | source)
XLA Modules:
  0.0 293.5 jit_solution(14642825721862563443)
XLA Ops:
  7.2 0.0 all-gather.6.cloned.1.call-start
  7.2 3.8 %sort.31 = (s32[256]{0:T(256)}, s32[256]{0:T(256)S(1)}) sort(s32[256]{0:T(256)} %param.7, s32[256]{0:T(256)S(1)} %iota.7), dimensions={0}, to_apply=%region_0.0 | sort | flops 2048 | bytes 4096 | tf_op jit(solution)/shard_map/jit(argsort)/sort | solution.py:18
  11.1 1.1 subtract_convert_fusion.4
  12.2 1.9 gather_fusion
  14.0 0.0 all-gather.6.cloned.1.call-update
  14.0 0.0 all-gather.8.cloned.1.call-start
  14.1 3.2 %sort.32 = (s32[256]{0:T(256)}, s32[256]{0:T(256)S(1)}) sort(s32[256]{0:T(256)S(1)} %get-tuple-element.7, s32[256]{0:T(256)S(1)} %iota.8), dimensions={0}, to_apply=%region_1.2 | sort | flops 2048 | bytes 4096 | tf_op jit(solution)/shard_map/jit(argsort)/sort | solution.py:19
  17.3 0.7 convert_element_type.19
  18.0 0.1 copy.11
  18.1 0.0 copy-start.1
  18.1 0.0 copy-start.3
  18.1 0.0 copy-start
  18.2 25.1 %all-gather.6.cloned.1.call-done = bf16[4,64,2048]{2,1,0:T(8,128)(2,1)} async-done(((bf16[4,64,512]{2,1,0:T(8,128)(2,1)}), bf16[4,64,2048]{2,1,0:T(8,128)(2,1)}) %all-gather.6.cloned.1.call-update) | async-done | bytes 1048592 | tf_op jit(solution)/shard_map/all_gather | solution.py:34
  43.3 6.4 %fusion.13 = f32[4,64,512]{2,1,0:T(8,128)S(1)} fusion(bf16[4,64,2048]{2,1,0:T(8,128)(2,1)} %all-gather.6.cloned.1.call-done, bf16[4,512,2048]{2,1,0:T(8,128)(2,1)} %param.9), kind=kOutput, calls=%fused_computation.56 | convolution fusion | flops 536870912 | bytes 9961472 | tf_op jit(solution)/shard_map/tas,tws->taw/dot_general | solution.py:32
  49.7 1.0 gather_fusion.1
  50.7 0.3 broadcast_in_dim.11
  51.0 0.1 fusion.12
  51.1 11.9 %psum.140 = f32[512]{0:T(512)S(1)} all-reduce(f32[512]{0:T(512)S(1)} %get-tuple-element.50), channel_id=1, replica_groups=mesh['agent'=8,'res'=4] {'agent'}, use_global_device_ids=true, to_apply=%region_3.4 | all-reduce | flops 512 | bytes 4096 | tf_op jit(solution)/shard_map/psum | solution.py:43
  63.0 0.0 copy-done.1
  63.0 0.0 copy-done.3
  63.0 0.6 multiply_reduce_fusion.9
  63.6 0.1 subtract_convert_fusion.3
  63.7 1.9 gather_fusion.2
  65.6 0.0 all-gather.8.cloned.1.call-update
  65.6 0.0 all-gather.10.cloned.1.call-start
  65.7 27.5 %all-gather.8.cloned.1.call-done = bf16[4,64,2048]{2,1,0:T(8,128)(2,1)} async-done(((bf16[4,64,512]{2,1,0:T(8,128)(2,1)}), bf16[4,64,2048]{2,1,0:T(8,128)(2,1)}) %all-gather.8.cloned.1.call-update) | async-done | bytes 1048592 | tf_op jit(solution)/shard_map/all_gather | solution.py:34
  93.1 6.4 %fusion.14 = f32[4,64,512]{2,1,0:T(8,128)S(1)} fusion(bf16[4,64,2048]{2,1,0:T(8,128)(2,1)} %all-gather.8.cloned.1.call-done, bf16[4,512,2048]{2,1,0:T(8,128)(2,1)} %param.9), kind=kOutput, calls=%fused_computation.57 | convolution fusion | flops 536870912 | bytes 9961472 | tf_op jit(solution)/shard_map/tas,tws->taw/dot_general | solution.py:32
  99.5 1.0 gather_fusion.3
  100.5 0.1 fusion.11
  100.6 11.9 %psum.141 = f32[512]{0:T(512)S(1)} all-reduce(f32[512]{0:T(512)S(1)} %get-tuple-element.48), channel_id=1, replica_groups=mesh['agent'=8,'res'=4] {'agent'}, use_global_device_ids=true, to_apply=%region_5.6 | all-reduce | flops 512 | bytes 4096 | tf_op jit(solution)/shard_map/psum | solution.py:43
  112.5 0.6 multiply_reduce_fusion.8
  113.1 0.1 subtract_convert_fusion.2
  113.2 1.9 gather_fusion.4
  115.0 0.0 all-gather.10.cloned.1.call-update
  115.1 0.0 all-gather.12.cloned.1.call-start
  115.1 27.5 %all-gather.10.cloned.1.call-done = bf16[4,64,2048]{2,1,0:T(8,128)(2,1)} async-done(((bf16[4,64,512]{2,1,0:T(8,128)(2,1)}), bf16[4,64,2048]{2,1,0:T(8,128)(2,1)}) %all-gather.10.cloned.1.call-update) | async-done | bytes 1048592 | tf_op jit(solution)/shard_map/all_gather | solution.py:34
  142.6 6.4 %fusion.15 = f32[4,64,512]{2,1,0:T(8,128)S(1)} fusion(bf16[4,64,2048]{2,1,0:T(8,128)(2,1)} %all-gather.10.cloned.1.call-done, bf16[4,512,2048]{2,1,0:T(8,128)(2,1)} %param.9), kind=kOutput, calls=%fused_computation.58 | convolution fusion | flops 536870912 | bytes 9961472 | tf_op jit(solution)/shard_map/tas,tws->taw/dot_general | solution.py:32
  148.9 1.0 gather_fusion.5
  149.9 0.1 fusion.10
  150.0 12.1 %psum.142 = f32[512]{0:T(512)S(1)} all-reduce(f32[512]{0:T(512)S(1)} %get-tuple-element.46), channel_id=1, replica_groups=mesh['agent'=8,'res'=4] {'agent'}, use_global_device_ids=true, to_apply=%region_7.8 | all-reduce | flops 512 | bytes 4096 | tf_op jit(solution)/shard_map/psum | solution.py:43
  162.1 0.6 multiply_reduce_fusion.7
  162.7 0.1 subtract_convert_fusion.1
  162.8 1.9 gather_fusion.6
  164.7 0.0 all-gather.12.cloned.1.call-update
  164.7 0.0 all-gather.14.cloned.1.call-start
  164.8 27.4 %all-gather.12.cloned.1.call-done = bf16[4,64,2048]{2,1,0:T(8,128)(2,1)} async-done(((bf16[4,64,512]{2,1,0:T(8,128)(2,1)}), bf16[4,64,2048]{2,1,0:T(8,128)(2,1)}) %all-gather.12.cloned.1.call-update) | async-done | bytes 1048592 | tf_op jit(solution)/shard_map/all_gather | solution.py:34
  192.2 6.4 %fusion.16 = f32[4,64,512]{2,1,0:T(8,128)S(1)} fusion(bf16[4,64,2048]{2,1,0:T(8,128)(2,1)} %all-gather.12.cloned.1.call-done, bf16[4,512,2048]{2,1,0:T(8,128)(2,1)} %param.9), kind=kOutput, calls=%fused_computation.59 | convolution fusion | flops 536870912 | bytes 9961472 | tf_op jit(solution)/shard_map/tas,tws->taw/dot_general | solution.py:32
  198.6 1.8 gather_fusion.7
  200.4 1.2 fusion.9
  201.5 11.9 %psum.143 = f32[512]{0:T(512)S(1)} all-reduce(f32[512]{0:T(512)S(1)} %get-tuple-element.44), channel_id=1, replica_groups=mesh['agent'=8,'res'=4] {'agent'}, use_global_device_ids=true, to_apply=%region_9.10 | all-reduce | flops 512 | bytes 4096 | tf_op jit(solution)/shard_map/psum | solution.py:43
  213.4 0.6 multiply_reduce_fusion.6
  214.0 0.1 subtract_convert_fusion
  214.1 1.9 gather_fusion.8
  216.0 0.0 all-gather.14.cloned.1.call-update
  218.6 24.9 %all-gather.14.cloned.1.call-done = bf16[4,64,2048]{2,1,0:T(8,128)(2,1)} async-done(((bf16[4,64,512]{2,1,0:T(8,128)(2,1)}), bf16[4,64,2048]{2,1,0:T(8,128)(2,1)}) %all-gather.14.cloned.1.call-update) | async-done | bytes 1048592 | tf_op jit(solution)/shard_map/all_gather | solution.py:34
  243.5 6.4 %fusion.17 = f32[4,64,512]{2,1,0:T(8,128)S(1)} fusion(bf16[4,64,2048]{2,1,0:T(8,128)(2,1)} %all-gather.14.cloned.1.call-done, bf16[4,512,2048]{2,1,0:T(8,128)(2,1)} %param.9), kind=kOutput, calls=%fused_computation.60 | convolution fusion | flops 536870912 | bytes 9961472 | tf_op jit(solution)/shard_map/tas,tws->taw/dot_general | solution.py:32
  249.9 1.8 gather_fusion.9
  251.7 2.8 multiply_reduce_fusion
  254.4 12.8 %all-reduce = (f32[512]{0:T(512)S(1)}, f32[]{:T(128)}, f32[]{:T(128)}, f32[]{:T(128)}, f32[]{:T(128)}, /*index=5*/f32[]{:T(128)}) all-reduce(f32[512]{0:T(512)S(1)} %get-tuple-element.14, f32[]{:T(128)} %get-tuple-element.13, f32[]{:T(128)} %get-tuple-element.12, ...), channel_id=1, replica_groups=mesh['agent'=8,'res'=4] {'agent'}, use_global_device_ids=true, to_apply=%region_11.12 | all-reduce | flops 517 | bytes 4136 | tf_op jit(solution)/shard_map/psum | solution.py:43
  267.3 0.6 multiply_reduce_fusion.5
  268.5 0.6 fusion
  269.1 10.0 %all-reduce.1 = (f32[]{:T(128)}, f32[]{:T(128)}, f32[]{:T(128)}, f32[]{:T(128)}, f32[]{:T(128)}, /*index=5*/f32[]{:T(128)}, f32[]{:T(128)}, f32[]{:T(128)}, f32[]{:T(128)}, f32[]{:T(128)}) all-reduce(f32[]{:T(128)S(6)} %mul.99, f32[]{:T(128)S(6)} %mul.100, f32[]{:T(128)S(6)} %mul.101, ...), channel_id=1, replica_groups=mesh['agent'=8,'res'=4] {'res'}, use_global_device_ids=true, to_apply=%region_13.14 | all-reduce | flops 10 | bytes 80 | tf_op jit(solution)/shard_map/psum | solution.py:48
  285.8 0.6 stack.41
  286.4 0.6 stack.47
  (12 shorter events, 0.0 us)
Async XLA Ops:
  7.2 36.1 %all-gather.6.cloned.1.call-start = ((), (), s32[]{:S(2)}) async-start(), calls=%async_computation | async-start | bytes 1310720 | tf_op jit(solution)/shard_map/all_gather | solution.py:34
  14.0 79.1 %all-gather.8.cloned.1.call-start = ((), (), s32[]{:S(2)}) async-start(), calls=%async_computation.1 | async-start | bytes 1310720 | tf_op jit(solution)/shard_map/all_gather | solution.py:34
  18.1 44.9 %copy-start.1 = (f32[512]{0:T(512)S(1)}, f32[512]{0:T(512)}, u32[]{:S(2)}) copy-start(f32[512]{0:T(512)} %param.10) | copy-start | bytes 6148
  18.1 44.9 %copy-start.3 = (f32[512]{0:T(512)S(1)}, f32[512]{0:T(512)}, u32[]{:S(2)}) copy-start(f32[512]{0:T(512)} %param.11) | copy-start | bytes 6148
  18.1 45.5 %copy-start = (f32[256,512]{1,0:T(8,128)S(1)}, f32[256,512]{1,0:T(8,128)}, u32[]{:S(2)}) copy-start(f32[256,512]{1,0:T(8,128)} %param.6) | copy-start | bytes 1572868
  65.6 77.0 %all-gather.10.cloned.1.call-start = ((), (), s32[]{:S(2)}) async-start(), calls=%async_computation.2 | async-start | bytes 1310720 | tf_op jit(solution)/shard_map/all_gather | solution.py:34
  115.1 77.2 %all-gather.12.cloned.1.call-start = ((), (), s32[]{:S(2)}) async-start(), calls=%async_computation.3 | async-start | bytes 1310720 | tf_op jit(solution)/shard_map/all_gather | solution.py:34
  164.7 78.8 %all-gather.14.cloned.1.call-start = ((), (), s32[]{:S(2)}) async-start(), calls=%async_computation.4 | async-start | bytes 1310720 | tf_op jit(solution)/shard_map/all_gather | solution.py:34
  267.9 19.1 %copy-start.2 = (f32[512]{0:T(512)}, f32[512]{0:T(512)S(1)}, u32[]{:S(2)}) copy-start(f32[512]{0:T(512)S(1)} %get-tuple-element.32) | copy-start | bytes 6148
Sparse Core Ops, SparseCore 0:
  14.2 29.0 all-gather.5
  65.7 27.3 all-gather.7
  115.2 27.3 all-gather.9
  164.8 27.3 all-gather.11
  216.1 27.3 all-gather.13
